TPU v7x, 32 devices: a whole 2x2x4 slice. The times are simulated.
32 devices in a mesh: ctx: 8 (over z, y), head: 4 (over x, core).
Axes of the slice: x: 2, y: 2, z: 4, core: 2. Of those that a mesh axis runs over, the one named last changes fastest.
Arguments:
- query: bfloat16 [8, 64, 576], P('ctx', 'head'), may hold values from -20 to 20
- cache: bfloat16 [32768, 576], P('ctx'), may hold values from -20 to 20
- cotangent: bfloat16 [8, 64, 512], P('ctx', 'head'), may hold values from -6 to 6
- positions: int32 [8], P('ctx'), may hold values from 0 to 262143
- visible: int32 [8], replicated, may hold values from 128 to 32768, as said below
Outputs:
- attention: bfloat16 [8, 64, 512], P('ctx', 'head')
- grad_query: float32 [8, 64, 576], P('ctx', 'head')
- grad_cache: bfloat16 [32768, 576], P('ctx')
Inputs may be any that keep to these rules, and one draw needn't show every extreme that they name: `visible`: each entry is a multiple of 128; some rollout token sees all 32768 prompt tokens.
All inputs are finite; a program needn't handle non-finite values.
Results may differ from a plain program's by a relative error of at most 0.01855.
Values may be sent and summed in bfloat16 or wider, within the bound.
No kernel may reach another device: no remote copies, remote signals or barrier semaphores. Data moves between devices by JAX's collectives and lax.ppermute only.
A program may use at most 128 MiB of HBM per device.

v0:
```python
import jax
import jax.numpy as jnp
import numpy as np
from jax import lax
from jax.sharding import PartitionSpec as P

softmax_scale = 192.0 ** (-0.5)
position_bits = 18
masked_value = -1e30


def rotation(positions, half_width):
    frequency = 10000.0 ** (-np.arange(half_width) / half_width)
    angles = np.outer(2.0 ** np.arange(position_bits), frequency)
    cosine_table = jnp.asarray(np.cos(angles), jnp.float32)
    sine_table = jnp.asarray(np.sin(angles), jnp.float32)
    cosines = jnp.ones((positions.shape[0], half_width), jnp.float32)
    sine_part = jnp.zeros((positions.shape[0], half_width), jnp.float32)
    for bit_index in range(position_bits):
        switch = (positions // 2**bit_index % 2).astype(jnp.float32)[:, None]
        step_cos = 1.0 + switch * (cosine_table[bit_index] - 1.0)
        step_sin = switch * sine_table[bit_index]
        cosines, sine_part = (
            cosines * step_cos - sine_part * step_sin,
            sine_part * step_cos + cosines * step_sin,
        )
    return (cosines[:, None, :], sine_part[:, None, :])


def rotate(tensor, cosines, sine_part, value_width, inverse):
    half_width = cosines.shape[-1]
    lower = tensor[..., value_width : value_width + half_width]
    upper = tensor[..., value_width + half_width :]
    if inverse:
        sine_part = -sine_part
    new_lower = lower * cosines - upper * sine_part
    new_upper = lower * sine_part + upper * cosines
    return jnp.concatenate([tensor[..., :value_width], new_lower, new_upper], axis=-1)


def body(query, cache, cotangent, positions, visible):
    value_width = cotangent.shape[-1]
    half_width = (query.shape[-1] - value_width) // 2
    extra_width = cache.shape[1] - value_width
    cosines, sine_part = rotation(positions, half_width)
    rotated = rotate(query.astype(jnp.float32), cosines, sine_part, value_width, False).astype(
        jnp.bfloat16
    )
    rotated, gradients = (
        lax.all_gather(rotated, "ctx", axis=0, tiled=True),
        lax.all_gather(cotangent, "ctx", axis=0, tiled=True),
    )
    block_rows = cache.shape[0]
    first_key = lax.axis_index("ctx") * block_rows
    key_index = first_key + jnp.arange(block_rows)
    allowed = key_index[None, None, :] < visible[:, None, None]
    scores = (
        jnp.einsum("thl,kl->thk", rotated, cache, preferred_element_type=jnp.float32)
        * softmax_scale
    )
    scores = jnp.where(allowed, scores, masked_value)
    local_peak = jnp.max(scores, axis=2)
    peak = lax.pmax(local_peak, "ctx")
    weights = jnp.where(allowed, jnp.exp(scores - peak[..., None]), 0.0)
    local_mass = jnp.sum(weights, axis=2)
    mass = lax.psum(local_mass, "ctx")
    probs = weights / mass[..., None]
    prob_low = probs.astype(jnp.bfloat16)
    values = cache[:, :value_width]
    attended = jnp.einsum("thk,kv->thv", prob_low, values, preferred_element_type=jnp.float32)
    attention = lax.psum_scatter(attended, "ctx", scatter_dimension=0, tiled=True).astype(
        jnp.bfloat16
    )
    grad_probs = jnp.einsum("thv,kv->thk", gradients, values, preferred_element_type=jnp.float32)
    local_delta = jnp.sum(prob_low.astype(jnp.float32) * grad_probs, axis=2)
    delta = lax.psum(local_delta, "ctx")
    grad_scores = (probs * (grad_probs - delta[..., None]) * softmax_scale).astype(jnp.bfloat16)
    grad_rotated = jnp.einsum("thk,kl->thl", grad_scores, cache, preferred_element_type=jnp.float32)
    grad_latent = jnp.einsum(
        "thk,thl->kl", grad_scores, rotated, preferred_element_type=jnp.float32
    )
    grad_value = jnp.einsum("thk,thv->kv", prob_low, gradients, preferred_element_type=jnp.float32)
    grad_latent = grad_latent + jnp.pad(grad_value, ((0, 0), (0, extra_width)))
    grad_cache = lax.psum(grad_latent, "head").astype(jnp.bfloat16)
    grad_rotated = lax.psum_scatter(grad_rotated, "ctx", scatter_dimension=0, tiled=True)
    grad_query = rotate(grad_rotated, cosines, sine_part, value_width, True)
    return (attention, grad_query, grad_cache)


def solution(mesh):
    placed = (P("ctx", "head", None), P("ctx", None), P("ctx", "head", None), P("ctx"), P())
    return jax.shard_map(
        body,
        mesh=mesh,
        in_specs=placed,
        out_specs=(P("ctx", "head", None), P("ctx", "head", None), P("ctx", None)),
        check_vma=False,
    )
```

profile of v0, /device:TPU:0, one launch (start us, length us, event | category | flops | bytes accessed | tf_op | source)
XLA Modules:
  0.0 339.2 jit_solution(13869444425280142998)
XLA Ops:
  7.2 0.0 reduce-scatter.3.cloned.1.call-start
  8.3 0.7 slice.130
  9.0 0.7 convert_element_type.83
  9.8 32.5 %all_gather.7 = bf16[8,16,512]{2,1,0:T(8,128)(2,1)S(1)} all-gather(bf16[1,16,512]{2,1,0:T(8,128)(2,1)} %param.9), channel_id=1, replica_groups=mesh['ctx'=8,'head'=4] {'ctx'}, dimensions={0}, use_global_device_ids=true | all-gather | bytes 147456 | tf_op jit(solution)/shard_map/all_gather | solution.py:51
  42.3 0.7 fusion.15
  43.0 0.7 fusion.18
  43.7 0.7 fusion.22
  44.5 0.7 fusion.26
  45.2 0.7 fusion.30
  46.0 0.7 fusion.34
  46.7 0.7 fusion.38
  47.5 0.7 fusion.42
  48.2 0.7 fusion.50
  49.0 0.7 fusion.49
  49.7 0.1 subtract_convert_fusion
  49.7 0.1 pad_maximum_fusion.1
  49.8 30.6 %all_gather.6 = bf16[8,16,576]{2,1,0:T(8,128)(2,1)S(1)} all-gather(bf16[1,16,576]{2,1,0:T(8,128)(2,1)S(1)} %pad_maximum_fusion.1), channel_id=1, replica_groups=mesh['ctx'=8,'head'=4] {'ctx'}, dimensions={0}, use_global_device_ids=true | all-gather | bytes 165888 | tf_op jit(solution)/shard_map/all_gather | solution.py:50
  80.4 0.7 broadcast_compare_fusion
  81.1 3.6 %fusion.69 = (f32[8,16]{1,0:T(8,128)S(1)}, f32[8,16,4096]{2,1,0:T(8,128)S(1)}) fusion(bf16[8,16,576]{2,1,0:T(8,128)(2,1)S(1)} %all_gather.6, bf16[4096,576]{0,1:T(8,128)(2,1)} %param.8, pred[8,4096]{1,0:T(8,128)(4,1)S(1)} %broadcast_compare_fusion), kind=kOutput, calls=%fused_computation.119 | convolution fusion | flops 605552512 | bytes 6996480 | tf_op jit(solution)/shard_map/thl,kl->thk/dot_general | solution.py:58
  84.8 21.4 %pmax.7 = f32[8,16]{1,0:T(8,128)S(1)} all-reduce(f32[8,16]{1,0:T(8,128)S(1)} %get-tuple-element.36), channel_id=1, replica_groups=mesh['ctx'=8,'head'=4] {'ctx'}, use_global_device_ids=true, to_apply=%region_1.2 | all-reduce | flops 128 | bytes 1024 | tf_op jit(solution)/shard_map/pmax | solution.py:63
  106.1 0.0 slice-start
  106.1 0.6 fusion.11
  106.7 17.1 %psum.21 = f32[8,16]{1,0:T(8,128)S(1)} all-reduce(f32[8,16]{1,0:T(8,128)S(1)} %fusion.11), channel_id=1, replica_groups=mesh['ctx'=8,'head'=4] {'ctx'}, use_global_device_ids=true, to_apply=%region_3.4 | all-reduce | flops 128 | bytes 1024 | tf_op jit(solution)/shard_map/psum | solution.py:66
  123.8 0.0 slice-start.1
  123.8 4.9 %multiply_reduce_fusion = (f32[8,16]{1,0:T(8,128)S(1)}, bf16[8,16,4096]{2,1,0:T(8,128)(2,1)S(1)}, f32[8,16,4096]{2,1,0:T(8,128)}) fusion(f32[8,16]{1,0:T(8,128)S(1)} %psum.21, f32[8,16,4096]{2,1,0:T(8,128)S(1)} %get-tuple-element.37, f32[8,16]{1,0:T(8,128)S(1)} %pmax.7, pred[8,4096]{1,0:T(8,128)(4,1)S(1)} %broadcast_compare_fusion, ...), kind=kOutput, calls=%fused_computation.14 | convolution fusion | flops 540540800 | bytes 9602560 | tf_op jit(solution)/shard_map/thv,kv->thk/dot_general | solution.py:74
  128.7 0.0 copy-start
  128.7 1.0 copy-done
  129.7 0.0 slice-done
  129.7 0.0 slice-done.1
  129.7 2.3 fusion.6
  132.0 0.0 reduce-scatter.3.cloned.1.call-update
  132.0 0.0 reduce-scatter.5.cloned.1.call-start
  132.1 19.1 %psum.22 = f32[8,16]{1,0:T(8,128)S(1)} all-reduce(f32[8,16]{1,0:T(8,128)S(1)} %get-tuple-element.7), channel_id=1, replica_groups=mesh['ctx'=8,'head'=4] {'ctx'}, use_global_device_ids=true, to_apply=%region_6.7 | all-reduce | flops 128 | bytes 1024 | tf_op jit(solution)/shard_map/psum | solution.py:76
  151.2 2.3 multiply_convert_fusion
  153.6 0.0 copy-start.1
  153.6 4.9 %fusion.1 = f32[8,16,576]{2,1,0:T(8,128)} fusion(bf16[8,16,4096]{2,1,0:T(8,128)(2,1)S(1)} %multiply_convert_fusion, bf16[4096,576]{0,1:T(8,128)(2,1)} %param.8), kind=kOutput, calls=%fused_computation.4 | convolution fusion | flops 603979776 | bytes 6062080 | tf_op jit(solution)/shard_map/thk,kl->thl/dot_general | solution.py:78
  158.5 0.0 reduce-scatter.5.cloned.1.call-update
  158.5 0.0 copy-done.1
  158.5 1.3 convolution_bitcast_fusion
  159.8 5.1 %bitcast_add_fusion = f32[4096,576]{0,1:T(8,128)} fusion(f32[4096,512]{0,1:T(8,128)S(1)} %convolution_bitcast_fusion, bf16[8,16,4096]{2,1,0:T(8,128)(2,1)S(1)} %multiply_convert_fusion, bf16[8,16,576]{2,1,0:T(8,128)(2,1)S(1)} %all_gather.6), kind=kOutput, calls=%fused_computation | convolution fusion | flops 606339072 | bytes 19021824 | tf_op jit(solution)/shard_map/thk,thl->kl/dot_general | solution.py:79
  164.9 163.8 %all-reduce.2 = bf16[4096,576]{0,1:T(8,128)(2,1)} all-reduce(f32[4096,576]{0,1:T(8,128)} %bitcast_add_fusion), channel_id=1, replica_groups=mesh['ctx'=8,'head'=4] {'head'}, use_global_device_ids=true, to_apply=%region_8.9 | all-reduce | flops 2359296 | bytes 14155776 | tf_op jit(solution)/shard_map/psum | solution.py:84
  328.7 0.0 reduce-scatter.3.cloned.1.call-done
  328.7 1.4 convert_element_type.103
  330.0 0.0 reduce-scatter.5.cloned.1.call-done
  330.0 0.8 slice.175
  330.8 0.9 multiply_subtract_fusion
  331.7 0.7 pad_maximum_fusion
  (2 shorter events, 0.0 us)
Async XLA Ops:
  7.2 321.5 %reduce-scatter.3.cloned.1.call-start = ((), (), s32[]{:S(2)}) async-start(), calls=%async_computation.2 | async-start | bytes 294912 | tf_op jit(solution)/shard_map/reduce_scatter | solution.py:71
  106.1 23.6 %slice-start = ((s8[4718592]{0:T(1024)(128)(4,1)}), s8[524288]{0:T(1024)(128)(4,1)S(1)}, s32[]{:S(2)}) async-start(s8[4718592]{0:T(1024)(128)(4,1)} %bitcast.51), calls=%async_computation.4 | async-start | bytes 1048576
  123.8 5.9 %slice-start.1 = ((s8[4718592]{0:T(1024)(128)(4,1)}), s8[4194304]{0:T(1024)(128)(4,1)S(1)}, s32[]{:S(2)}) async-start(s8[4718592]{0:T(1024)(128)(4,1)} %bitcast.51), calls=%async_computation.5 | async-start | bytes 8388608
  128.7 1.0 copy-start
  132.0 198.0 %reduce-scatter.5.cloned.1.call-start = ((), (), s32[]{:S(2)}) async-start(), calls=%async_computation.3 | async-start | bytes 368640 | tf_op jit(solution)/shard_map/reduce_scatter | solution.py:85
  153.6 4.9 %copy-start.1 = (bf16[8,16,4096]{2,1,0:T(8,128)(2,1)S(1)}, bf16[8,16,4096]{2,1,0:T(8,128)(2,1)}, u32[]{:S(2)}) copy-start(bf16[8,16,4096]{2,1,0:T(8,128)(2,1)} %copy-done) | copy-start | bytes 3145732
Sparse Core Ops, SparseCore 0:
  132.1 60.7 reduce-scatter.2
  196.2 61.2 reduce-scatter.4
where the time goes:
time: 340 us; the launch traced here: 339 us
  blocking collectives  285 us (84%)
  matrix products  22.1 us (6%)
  between operations  15.2 us (4%)
  other arithmetic  14.8 us (4%)
    psum x1, blocking collectives, body(): grad_cache = lax.psum(grad_latent, 'head').astype(jnp.bfloat16)  164 us
    all_gather x1, blocking collectives, body(): lax.all_gather(cotangent, 'ctx', axis=0, tiled=True)  32.5 us
    all_gather x1, blocking collectives, body(): lax.all_gather(rotated, 'ctx', axis=0, tiled=True)  30.6 us
    pmax x1, blocking collectives, body(): peak = lax.pmax(local_peak, 'ctx')  21.4 us
    psum x1, blocking collectives, body(): delta = lax.psum(local_delta, 'ctx')  19.1 us
    psum x1, blocking collectives, body(): mass = lax.psum(local_mass, 'ctx')  17.1 us
  transfers between devices with their start and end apart: 2, of which 0 were waited for; matrix products, arithmetic and copies ran while one was open for 4% of the time, Pallas kernels for 0%

commit v1 on v0

--- a/solution.py
+++ b/solution.py
@@ -7,6 +7,12 @@
 softmax_scale = 192.0 ** (-0.5)
 position_bits = 18
 masked_value = -1e30
+
+
+def add_all(x, name):
+    terms = lax.all_gather(x, name, axis=0, tiled=False)
+    summed = terms.sum(axis=0)
+    return summed
 
 
 def rotation(positions, half_width):
@@ -81,7 +87,7 @@
     )
     grad_value = jnp.einsum("thk,thv->kv", prob_low, gradients, preferred_element_type=jnp.float32)
     grad_latent = grad_latent + jnp.pad(grad_value, ((0, 0), (0, extra_width)))
-    grad_cache = lax.psum(grad_latent, "head").astype(jnp.bfloat16)
+    grad_cache = add_all(grad_latent, "head").astype(jnp.bfloat16)
     grad_rotated = lax.psum_scatter(grad_rotated, "ctx", scatter_dimension=0, tiled=True)
     grad_query = rotate(grad_rotated, cosines, sine_part, value_width, True)
     return (attention, grad_query, grad_cache)

time: 340 us -> 471 us (1.39)
  waiting for transfers between devices: 0.04 us -> 221 us
  blocking collectives: 285 us -> 121 us
  local copies, waits for them, and re-layouts: 2.48 us -> 46.8 us
  other arithmetic: 14.8 us -> 42.3 us
    psum x1 -> x0, blocking collectives: 164 us -> none  [body(): grad_cache = lax.psum(grad_latent, 'head').astype(jnp.bfloat16)]
    all_gather x0 -> x1, waiting for transfers between devices: none -> 129 us  [add_all(): terms = lax.all_gather(x, name, axis=0, tiled=False)]
    reduce_scatter x1, waiting for transfers between devices: 0.01 us -> 63.7 us  [body(): lax.psum_scatter(grad_rotated, 'ctx', scatter_dimension=0, tiled=True)]
    all_gather x0 -> x1, local copies, waits for them, and re-layouts: none -> 44.4 us  [add_all(): terms = lax.all_gather(x, name, axis=0, tiled=False)]
    reduce_scatter x1, waiting for transfers between devices: 0.01 us -> 27.8 us  [body(): lax.psum_scatter(attended, 'ctx', scatter_dimension=0, tiled=True)]
    reduce_sum x0 -> x1, other arithmetic: none -> 27.5 us  [add_all(): summed = terms.sum(axis=0)]
  transfers between devices with their start and end apart: 2 -> 3, of which waited for: 0 -> 3; matrix products, arithmetic and copies ran while one was open for 4% -> 4% of each run, Pallas kernels for 0% -> 0%
where the time goes in v1:
time: 471 us; the launch traced here: 470 us
  waiting for transfers between devices  221 us (47%)
  blocking collectives  121 us (26%)
  local copies, waits for them, and re-layouts  46.8 us (10%)
  other arithmetic  42.3 us (9%)
  matrix products  22 us (5%)
  between operations  16.7 us (4%)
    all_gather x1, waiting for transfers between devices, add_all(): terms = lax.all_gather(x, name, axis=0, tiled=False)  129 us
    reduce_scatter x1, waiting for transfers between devices, body(): lax.psum_scatter(grad_rotated, 'ctx', scatter_dimension=0, tiled=True)  63.7 us
    all_gather x1, local copies, waits for them, and re-layouts, add_all(): terms = lax.all_gather(x, name, axis=0, tiled=False)  44.4 us
    all_gather x1, blocking collectives, body(): lax.all_gather(cotangent, 'ctx', axis=0, tiled=True)  32.5 us
    all_gather x1, blocking collectives, body(): lax.all_gather(rotated, 'ctx', axis=0, tiled=True)  30.6 us
    reduce_scatter x1, waiting for transfers between devices, body(): lax.psum_scatter(attended, 'ctx', scatter_dimension=0, tiled=True)  27.8 us
    reduce_sum x1, other arithmetic, add_all(): summed = terms.sum(axis=0)  27.5 us
    pmax x1, blocking collectives, body(): peak = lax.pmax(local_peak, 'ctx')  21.4 us
  transfers between devices with their start and end apart: 3, of which 3 were waited for; matrix products, arithmetic and copies ran while one was open for 4% of the time, Pallas kernels for 0%

profile of v1, /device:TPU:0, one launch (start us, length us, event | category | flops | bytes accessed | tf_op | source)
XLA Modules:
  0.0 469.7 jit_solution(1641697301060233314)
XLA Ops:
  8.0 0.0 reduce-scatter.3.cloned.1.call-start
  9.2 0.7 slice.130
  9.9 0.7 convert_element_type.83
  10.6 32.5 %all_gather.13 = bf16[8,16,512]{2,1,0:T(8,128)(2,1)S(1)} all-gather(bf16[1,16,512]{2,1,0:T(8,128)(2,1)} %param.9), channel_id=1, replica_groups=mesh['ctx'=8,'head'=4] {'ctx'}, dimensions={0}, use_global_device_ids=true | all-gather | bytes 147456 | tf_op jit(solution)/shard_map/all_gather | solution.py:57
  43.2 0.7 fusion.15
  43.9 0.7 fusion.18
  44.6 0.7 fusion.22
  45.3 0.7 fusion.26
  46.1 0.7 fusion.30
  46.8 0.7 fusion.34
  47.6 0.7 fusion.38
  48.3 0.7 fusion.42
  49.1 0.7 fusion.50
  49.8 0.7 fusion.49
  50.5 0.1 subtract_convert_fusion
  50.6 0.1 pad_maximum_fusion.1
  50.7 30.6 %all_gather.12 = bf16[8,16,576]{2,1,0:T(8,128)(2,1)S(1)} all-gather(bf16[1,16,576]{2,1,0:T(8,128)(2,1)S(1)} %pad_maximum_fusion.1), channel_id=1, replica_groups=mesh['ctx'=8,'head'=4] {'ctx'}, dimensions={0}, use_global_device_ids=true | all-gather | bytes 165888 | tf_op jit(solution)/shard_map/all_gather | solution.py:56
  81.2 0.7 broadcast_compare_fusion
  82.0 3.6 fusion.69
  85.6 21.4 %pmax.7 = f32[8,16]{1,0:T(8,128)S(1)} all-reduce(f32[8,16]{1,0:T(8,128)S(1)} %get-tuple-element.36), channel_id=1, replica_groups=mesh['ctx'=8,'head'=4] {'ctx'}, use_global_device_ids=true, to_apply=%region_1.2 | all-reduce | flops 128 | bytes 1024 | tf_op jit(solution)/shard_map/pmax | solution.py:69
  107.0 0.6 fusion.11
  107.5 17.1 %psum.14 = f32[8,16]{1,0:T(8,128)S(1)} all-reduce(f32[8,16]{1,0:T(8,128)S(1)} %fusion.11), channel_id=1, replica_groups=mesh['ctx'=8,'head'=4] {'ctx'}, use_global_device_ids=true, to_apply=%region_3.4 | all-reduce | flops 128 | bytes 1024 | tf_op jit(solution)/shard_map/psum | solution.py:72
  124.7 4.9 %multiply_reduce_fusion = (f32[8,16]{1,0:T(8,128)S(1)}, bf16[8,16,4096]{2,1,0:T(8,128)(2,1)S(1)}, f32[8,16,4096]{2,1,0:T(8,128)}) fusion(f32[8,16]{1,0:T(8,128)S(1)} %psum.14, f32[8,16,4096]{2,1,0:T(8,128)S(1)} %get-tuple-element.37, f32[8,16]{1,0:T(8,128)S(1)} %pmax.7, pred[8,4096]{1,0:T(8,128)(4,1)S(1)} %broadcast_compare_fusion, ...), kind=kOutput, calls=%fused_computation.14 | convolution fusion | flops 540540800 | bytes 9602560 | tf_op jit(solution)/shard_map/thv,kv->thk/dot_general | solution.py:80
  129.5 1.0 copy-done
  130.5 0.0 slice-done
  130.5 0.0 slice-done.1
  130.5 2.3 fusion.6
  132.8 0.0 reduce-scatter.3.cloned.1.call-update
  132.8 0.0 reduce-scatter.5.cloned.1.call-start
  132.9 19.1 %psum.15 = f32[8,16]{1,0:T(8,128)S(1)} all-reduce(f32[8,16]{1,0:T(8,128)S(1)} %get-tuple-element.7), channel_id=1, replica_groups=mesh['ctx'=8,'head'=4] {'ctx'}, use_global_device_ids=true, to_apply=%region_6.7 | all-reduce | flops 128 | bytes 1024 | tf_op jit(solution)/shard_map/psum | solution.py:82
  152.0 2.3 multiply_convert_fusion
  154.4 0.0 copy-start.1
  154.4 4.9 %fusion.1 = f32[8,16,576]{2,1,0:T(8,128)} fusion(bf16[8,16,4096]{2,1,0:T(8,128)(2,1)S(1)} %multiply_convert_fusion, bf16[4096,576]{0,1:T(8,128)(2,1)} %param.8), kind=kOutput, calls=%fused_computation.4 | convolution fusion | flops 603979776 | bytes 6062080 | tf_op jit(solution)/shard_map/thk,kl->thl/dot_general | solution.py:84
  159.3 0.0 reduce-scatter.5.cloned.1.call-update
  159.3 0.2 all-gather.3.cloned.1.call-start
  159.6 0.0 copy-done.1
  159.6 1.3 convolution_bitcast_fusion
  160.9 5.1 %bitcast_add_fusion = f32[4096,576]{0,1:T(8,128)} fusion(f32[4096,512]{0,1:T(8,128)S(1)} %convolution_bitcast_fusion, bf16[8,16,4096]{2,1,0:T(8,128)(2,1)S(1)} %multiply_convert_fusion, bf16[8,16,576]{2,1,0:T(8,128)(2,1)S(1)} %all_gather.12), kind=kOutput, calls=%fused_computation | convolution fusion | flops 606339072 | bytes 19021824 | tf_op jit(solution)/shard_map/thk,thl->kl/dot_general | solution.py:85
  165.9 0.0 all-gather.3.cloned.1.call-update
  165.9 27.8 %reduce-scatter.3.cloned.1.call-done = f32[1,16,512]{2,1,0:T(8,128)} async-done(((f32[8,16,512]{2,1,0:T(8,128)}), f32[1,16,512]{2,1,0:T(8,128)}) %reduce-scatter.3.cloned.1.call-update) | async-done | bytes 32784 | tf_op jit(solution)/shard_map/reduce_scatter | solution.py:77
  193.8 1.4 convert_element_type.103
  195.1 63.7 %reduce-scatter.5.cloned.1.call-done = f32[1,16,576]{2,1,0:T(8,128)} async-done(((f32[8,16,576]{2,1,0:T(8,128)}), f32[1,16,576]{2,1,0:T(8,128)}) %reduce-scatter.5.cloned.1.call-update) | async-done | bytes 36880 | tf_op jit(solution)/shard_map/reduce_scatter | solution.py:91
  258.8 0.8 slice.175
  259.6 0.8 multiply_subtract_fusion
  260.4 0.7 pad_maximum_fusion
  261.1 129.3 %all-gather.3.cloned.1.call-done = f32[16384,576]{0,1:T(8,128)} async-done(((f32[4096,576]{0,1:T(8,128)}), f32[16384,576]{0,1:T(8,128)}) %all-gather.3.cloned.1.call-update) | async-done | bytes 37748752 | tf_op jit(solution)/shard_map/all_gather | solution.py:13
  390.4 44.4 %reshape.294 = f32[4,4096,576]{1,0,2:T(4,128)} reshape(f32[16384,576]{0,1:T(8,128)} %all-gather.3.cloned.1.call-done) | data formatting | bytes 75497472 | tf_op jit(solution)/shard_map/all_gather | solution.py:13
  434.8 27.5 %reduce_sum.29 = bf16[4096,576]{0,1:T(8,128)(2,1)} reduce(f32[4,4096,576]{1,0,2:T(4,128)} %reshape.294, f32[]{:T(128)} %constant.447.clone.1), dimensions={0}, to_apply=%region_8.9 | reduce | flops 7077888 | bytes 42467332 | tf_op jit(solution)/shard_map/reduce_sum | solution.py:14
  (5 shorter events, 0.0 us)
Async XLA Ops:
  8.0 185.8 %reduce-scatter.3.cloned.1.call-start = ((), (), s32[]{:S(2)}) async-start(), calls=%async_computation.2 | async-start | bytes 294912 | tf_op jit(solution)/shard_map/reduce_scatter | solution.py:77
  107.0 23.6 %slice-start = ((s8[4718592]{0:T(1024)(128)(4,1)}), s8[524288]{0:T(1024)(128)(4,1)S(1)}, s32[]{:S(2)}) async-start(s8[4718592]{0:T(1024)(128)(4,1)} %bitcast.53), calls=%async_computation.5 | async-start | bytes 1048576
  124.7 5.8 %slice-start.1 = ((s8[4718592]{0:T(1024)(128)(4,1)}), s8[4194304]{0:T(1024)(128)(4,1)S(1)}, s32[]{:S(2)}) async-start(s8[4718592]{0:T(1024)(128)(4,1)} %bitcast.53), calls=%async_computation.6 | async-start | bytes 8388608
  129.5 1.0 copy-start
  132.8 126.0 %reduce-scatter.5.cloned.1.call-start = ((), (), s32[]{:S(2)}) async-start(), calls=%async_computation.3 | async-start | bytes 368640 | tf_op jit(solution)/shard_map/reduce_scatter | solution.py:91
  154.4 5.2 %copy-start.1 = (bf16[8,16,4096]{2,1,0:T(8,128)(2,1)S(1)}, bf16[8,16,4096]{2,1,0:T(8,128)(2,1)}, u32[]{:S(2)}) copy-start(bf16[8,16,4096]{2,1,0:T(8,128)(2,1)} %copy-done) | copy-start | bytes 3145732
  159.3 231.1 %all-gather.3.cloned.1.call-start = ((), (), s32[]{:S(2)}) async-start(), calls=%async_computation.4 | async-start | bytes 47185920 | tf_op jit(solution)/shard_map/all_gather | solution.py:13
Sparse Core Ops, SparseCore 0:
  133.0 60.7 reduce-scatter.2
  197.6 61.1 reduce-scatter.4
Sparse Core Ops, SparseCore 1:
  166.0 224.3 all-gather.2
